TPU v7x, 32 devices: a whole 2x2x4 slice. The times are simulated.
32 devices in a mesh: box: 32 (over z, y, x, core).
Axes of the slice: x: 2, y: 2, z: 4, core: 2. Of those that a mesh axis runs over, the one named last changes fastest.
Arguments:
- fine_multipoles: bfloat16 [152, 16384], P(None, 'box'), may hold values from -6 to 6
- present: int32 [16384], P('box'), may hold values from 0 to 1, as said below
- m2m_ops: bfloat16 [8, 152, 152], replicated, may hold values from -0.15625 to 0.15625
- m2l_ops: bfloat16 [316, 152, 152], replicated, may hold values from -0.0390625 to 0.0390625
- l2l_ops: bfloat16 [8, 152, 152], replicated, may hold values from -0.5 to 0.5
Outputs:
- fine_locals: float32 [152, 16384], P(None, 'box')
Inputs may be any that keep to these rules, and one draw needn't show every extreme that they name: `present`: the column of fine_multipoles of a box marked 0 holds no data and is not read.
All inputs are finite; a program needn't handle non-finite values.
Results may differ from a plain program's by a relative error of at most 0.0027.
Values may be sent and summed in bfloat16 or wider, within the bound.
A program may use at most 384 MiB of HBM per device.

v0:
```python
import functools

import jax
import jax.numpy as jnp
import numpy as np
from jax import lax
from jax.experimental import pallas as pl
from jax.experimental.pallas import tpu as pltpu
from jax.sharding import PartitionSpec as P

PAD = 16
NT_DIMS = (((1,), (1,)), ((), ()))


def offsets_table():
    entries = []
    for u in range(-3, 4):
        for v in range(-3, 4):
            for w in range(-3, 4):
                if max(abs(u), abs(v), abs(w)) >= 2:
                    entries.append((u, v, w))
    return entries


def coords_of(number, bit_count):
    out = [0, 0, 0]
    for i in range(bit_count):
        out[i % 3] |= (number >> i & 1) << (i // 3)
    return out


def extents(bit_count):
    return [2 ** len([i for i in range(bit_count) if i % 3 == a]) for a in range(3)]


def kind(o):
    return {-3: 0, 3: 2}.get(o, 1)


def classes_of(kinds):
    allowed = {0: (1,), 1: (0, 1), 2: (0,)}
    return [
        k
        for k in range(8)
        if all((k >> a & 1) in allowed[kinds[a]] for a in range(3))
    ]


def build_tables():
    offsets = offsets_table()
    rows, starts, slabs = [], [], []
    for u in range(-3, 4):
        members = [t for t, o in enumerate(offsets) if o[0] == u]
        slabs.append((members[0], len(members)))
        for kv in range(3):
            for kw in range(3):
                starts.append(len(rows))
                for t in members:
                    o = offsets[t]
                    if kind(o[1]) != kv or kind(o[2]) != kw:
                        continue
                    entry = [t]
                    for k in classes_of((kind(u), kv, kw)):
                        d, child = 0, 0
                        for a in range(3):
                            s = o[a] + (k >> a & 1)
                            child |= (s & 1) << a
                            d = d * 3 + (s >> 1) + 1
                        entry.append(d * 8 + child)
                    rows.append(entry + [0] * (9 - len(entry)))
    starts.append(len(rows))
    return np.array(rows, np.int32).reshape(-1), np.array(starts, np.int32), slabs


def selector(bit_count, pad):
    ex = extents(bit_count)
    count = 2**bit_count
    rows = max(count, pad)
    sel = np.zeros((27, rows, (ex[0] + 2) * (ex[1] + 2) * (ex[2] + 2)), np.float32)
    for c in range(count):
        x = coords_of(c, bit_count)
        r = (c & 7) * (count // 8) + (c >> 3) if count >= 64 else c
        for d in range(27):
            s = [x[0] + d // 9, x[1] + d // 3 % 3, x[2] + d % 3]
            sel[d, r, (s[0] * (ex[1] + 2) + s[1]) * (ex[2] + 2) + s[2]] = 1
    return sel.reshape(27 * rows, -1)


def far_kernel(
    slabs, nf, nc, tab_ref, start_ref, fine_ref, coarse_ref, sf_ref, sc_ref, l2l_ref, m2l_ref,
    out_ref, ops, win, acc, sems
):
    copies = []
    for i, (first, size) in enumerate(slabs):
        copy = pltpu.make_async_copy(
            m2l_ref.at[pl.ds(first, size)], ops.at[pl.ds(first, size)], sems.at[i]
        )
        copy.start()
        copies.append(copy)
    acc[...] = jnp.zeros_like(acc)
    points = fine_ref.shape[-1]

    def build(j, carry):
        f = fine_ref[j]
        c = coarse_ref[j]
        for d in range(27):
            win[d * 8 + j, 0:nf, :] = jnp.dot(
                sf_ref[d * nf : (d + 1) * nf, :], f, preferred_element_type=jnp.float32
            ).astype(jnp.bfloat16)
            win[d * 8 + j, nf : nf + PAD, :] = jnp.dot(
                sc_ref[d * PAD : (d + 1) * PAD, :], c, preferred_element_type=jnp.float32
            ).astype(jnp.bfloat16)
        return carry

    lax.fori_loop(0, 8, build, 0)
    rows = nf + PAD

    def slab(i, ku):
        for kv in range(3):
            for kw in range(3):
                ks = classes_of((ku, kv, kw))

                def step(n, carry, ks=ks):
                    op = ops[tab_ref[n * 9]]
                    lhs = jnp.concatenate(
                        [win[tab_ref[n * 9 + 1 + e]] for e in range(len(ks))], axis=0
                    )
                    res = lax.dot_general(lhs, op, NT_DIMS, preferred_element_type=jnp.float32)
                    for e, k in enumerate(ks):
                        acc[k] += res[e * rows : (e + 1) * rows]
                    return carry

                at = i * 9 + kv * 3 + kw
                lax.fori_loop(start_ref[at], start_ref[at + 1], step, 0)

    copies[0].wait()
    slab(0, 0)
    for i in range(1, 6):
        copies[i].wait()

    def inner(i, carry):
        slab(i, 1)
        return carry

    lax.fori_loop(1, 6, inner, 0)
    copies[6].wait()
    slab(6, 2)

    down = jnp.concatenate([acc[k, nf : nf + nc, :] for k in range(8)], axis=0).astype(jnp.bfloat16)
    for k in range(8):
        out_ref[k] = acc[k, 0:nf, :] + lax.dot_general(
            down, l2l_ref[k], NT_DIMS, preferred_element_type=jnp.float32
        )


def far_field(fine, coarse, m2l_ops, l2l_ops, nf, nc, local_bits):
    tab, starts, slabs = build_tables()
    points = fine.shape[-1]
    sf = jnp.asarray(selector(local_bits - 3, 0), jnp.bfloat16)
    sc = jnp.asarray(selector(local_bits - 6, PAD), jnp.bfloat16)
    vmem = pl.BlockSpec(memory_space=pltpu.VMEM)
    smem = pl.BlockSpec(memory_space=pltpu.SMEM)
    return pl.pallas_call(
        functools.partial(far_kernel, slabs, nf, nc),
        out_shape=jax.ShapeDtypeStruct((8, nf, points), jnp.float32),
        in_specs=[smem, smem, vmem, vmem, vmem, vmem, vmem, pl.BlockSpec(memory_space=pl.ANY)],
        out_specs=vmem,
        scratch_shapes=[
            pltpu.VMEM(m2l_ops.shape, jnp.bfloat16),
            pltpu.VMEM((27 * 8, nf + PAD, points), jnp.bfloat16),
            pltpu.VMEM((8, nf + PAD, points), jnp.float32),
            pltpu.SemaphoreType.DMA((len(slabs),)),
        ],
        compiler_params=pltpu.CompilerParams(vmem_limit_bytes=60 * 2**20),
        name="far_field",
    )(jnp.asarray(tab), jnp.asarray(starts), fine, coarse, sf, sc, l2l_ops, m2l_ops)


def to_grid(boxes, bit_count):
    lead, count, points = boxes.shape
    bitwise = boxes.reshape((lead,) + (2,) * bit_count + (points,))
    order = [0]
    for a in range(3):
        order += [bit_count - i for i in range(bit_count) if i % 3 == a][::-1]
    return bitwise.transpose(order + [bit_count + 1]).reshape([lead] + extents(bit_count) + [points])


def neighbours(devices, device_bits, local_bits, axis):
    members = [p for p in range(device_bits) if (local_bits + p) % 3 == axis]
    pairs = []
    for i in range(devices):
        coord = sum((i >> p & 1) << n for n, p in enumerate(members))
        if coord + 1 < 2 ** len(members):
            j = i
            for n, p in enumerate(members):
                j = j & ~(1 << p) | ((coord + 1) >> n & 1) << p
            pairs.append((i, j))
    return pairs


def exchange(grids, devices, device_bits, local_bits):
    for axis in range(3):
        up = neighbours(devices, device_bits, local_bits, axis)
        down = [(j, i) for i, j in up]
        dim = axis + 1

        def faces(at_top):
            cut = []
            for g in grids:
                s = g.shape[dim] - 1 if at_top else 0
                face = lax.slice_in_dim(g, s, s + 1, axis=dim)
                cut.append(face.reshape(g.shape[0], -1, g.shape[-1]))
            return jnp.concatenate(cut, axis=1)

        below = lax.ppermute(faces(True), "box", up)
        above = lax.ppermute(faces(False), "box", down)
        out, at = [], 0
        for g in grids:
            shape = list(g.shape)
            shape[dim] = 1
            size = shape[1] * shape[2] * shape[3]
            out.append(
                jnp.concatenate(
                    [
                        below[:, at : at + size].reshape(shape),
                        g,
                        above[:, at : at + size].reshape(shape),
                    ],
                    axis=dim,
                )
            )
            at += size
        grids = out
    return grids


def shards(fine_multipoles, present, m2m_ops, m2l_ops, l2l_ops):
    points, width = fine_multipoles.shape
    local_bits = width.bit_length() - 1
    devices = lax.axis_size("box")
    device_bits = devices.bit_length() - 1
    nf, nc = width // 8, width // 64
    masked = jnp.where(present[None, :] > 0, fine_multipoles, jnp.zeros_like(fine_multipoles))
    fine = masked.reshape(points, nf, 8).transpose(2, 1, 0)
    coarse = jnp.einsum(
        "kcq,kpq->cp", fine, m2m_ops, preferred_element_type=jnp.float32
    ).astype(jnp.bfloat16)
    coarse = coarse.reshape(nc, 8, points).transpose(1, 0, 2)
    grids = exchange(
        [to_grid(fine, local_bits - 3), to_grid(coarse, local_bits - 6)],
        devices, device_bits, local_bits,
    )
    flat = [g.reshape(8, -1, points) for g in grids]
    rows = far_field(flat[0], flat[1], m2l_ops, l2l_ops, nf, nc, local_bits)
    out = rows.reshape(8, 8, nc, points).transpose(3, 2, 1, 0).reshape(points, width)
    return jnp.where(present[None, :] > 0, out, 0.0)


def solution(mesh):
    in_specs = (P(None, "box"), P("box"), P(), P(), P())
    out_specs = P(None, "box")
    return jax.shard_map(shards, mesh=mesh, in_specs=in_specs, out_specs=out_specs, check_vma=False)
```

profile of v0, /device:TPU:24, one launch (start us, length us, event | category | flops | bytes accessed | tf_op | source)
XLA Modules:
  0.0 150.2 jit_solution(14268016348868005898)
XLA Ops:
  0.0 0.7 broadcast_compare_fusion
  0.8 1.0 copy.26
  1.8 0.1 fusion.7
  1.9 0.1 broadcast_select_fusion
  2.1 0.3 fusion
  2.5 1.9 %collective-permute-start.1 = (bf16[8,20,152]{2,0,1:T(8,128)(2,1)S(1)}, bf16[8,20,152]{2,0,1:T(8,128)(2,1)S(1)}, u32[]{:S(2)}, u32[]{:S(2)}) collective-permute-start(bf16[8,20,152]{2,0,1:T(8,128)(2,1)S(1)} %pad_maximum_fusion.16), channel_id=1, source_target_pairs={{1,0},{8,1},{3,2},{10,3},{5,4},{12,5},{7,6},{14,7},{9,8},{11,10},{... | collective-permute-start | bytes 145928 | tf_op jit(solution)/shard_map/ppermute | solution.py:216
  4.5 2.4 %collective-permute-start = (bf16[8,20,152]{2,0,1:T(8,128)(2,1)S(1)}, bf16[8,20,152]{2,0,1:T(8,128)(2,1)S(1)}, u32[]{:S(2)}, u32[]{:S(2)}) collective-permute-start(bf16[8,20,152]{2,0,1:T(8,128)(2,1)S(1)} %pad_maximum_fusion.15), channel_id=1, source_target_pairs={{0,1},{1,8},{2,3},{3,10},{4,5},{5,12},{6,7},{7,14},{8,9},{10,11},{... | collective-permute-start | bytes 145928 | tf_op jit(solution)/shard_map/ppermute | solution.py:215
  6.9 3.3 %collective-permute-done = bf16[8,20,152]{2,0,1:T(8,128)(2,1)S(1)} collective-permute-done((bf16[8,20,152]{2,0,1:T(8,128)(2,1)S(1)}, bf16[8,20,152]{2,0,1:T(8,128)(2,1)S(1)}, u32[]{:S(2)}, u32[]{:S(2)}) %collective-permute-start) | collective-permute-done | bytes 48672 | tf_op jit(solution)/shard_map/ppermute | solution.py:215
  10.4 3.2 %collective-permute-start.3 = (bf16[8,32,152]{2,0,1:T(8,128)(2,1)S(1)}, bf16[8,32,152]{2,0,1:T(8,128)(2,1)S(1)}, u32[]{:S(2)}, u32[]{:S(2)}) collective-permute-start(bf16[8,32,152]{2,0,1:T(8,128)(2,1)S(1)} %pad_maximum_fusion.10), channel_id=1, source_target_pairs={{2,0},{3,1},{16,2},{17,3},{6,4},{7,5},{20,6},{21,7},{10,8},{11,9},... | collective-permute-start | bytes 233480 | tf_op jit(solution)/shard_map/ppermute | solution.py:216
  13.6 2.7 %collective-permute-start.2 = (bf16[8,32,152]{2,0,1:T(8,128)(2,1)S(1)}, bf16[8,32,152]{2,0,1:T(8,128)(2,1)S(1)}, u32[]{:S(2)}, u32[]{:S(2)}) collective-permute-start(bf16[8,32,152]{2,0,1:T(8,128)(2,1)S(1)} %pad_maximum_fusion.9), channel_id=1, source_target_pairs={{0,2},{1,3},{2,16},{3,17},{4,6},{5,7},{6,20},{7,21},{8,10},{9,11},... | collective-permute-start | bytes 233480 | tf_op jit(solution)/shard_map/ppermute | solution.py:215
  16.3 1.0 collective-permute-done.3
  17.3 5.9 %collective-permute-done.2 = bf16[8,32,152]{2,0,1:T(8,128)(2,1)S(1)} collective-permute-done((bf16[8,32,152]{2,0,1:T(8,128)(2,1)S(1)}, bf16[8,32,152]{2,0,1:T(8,128)(2,1)S(1)}, u32[]{:S(2)}, u32[]{:S(2)}) %collective-permute-start.2) | collective-permute-done | bytes 77856 | tf_op jit(solution)/shard_map/ppermute | solution.py:215
  23.3 0.1 pad_maximum_fusion.8
  23.4 1.3 collective-permute-start.5
  24.8 4.6 %collective-permute-start.4 = (bf16[8,52,152]{2,0,1:T(8,128)(2,1)S(1)}, bf16[8,52,152]{2,0,1:T(8,128)(2,1)S(1)}, u32[]{:S(2)}, u32[]{:S(2)}) collective-permute-start(bf16[8,52,152]{2,0,1:T(8,128)(2,1)S(1)} %pad_maximum_fusion.2), channel_id=1, source_target_pairs={{0,4},{1,5},{2,6},{3,7},{8,12},{9,13},{10,14},{11,15},{16,20},{17,... | collective-permute-start | bytes 379400 | tf_op jit(solution)/shard_map/ppermute | solution.py:215
  29.3 37.1 %copy.43.m2l_ref = bf16[316,152,152]{2,1,0:T(8,128)(2,1)} copy(bf16[316,152,152]{0,2,1:T(8,128)(2,1)} %param.12) | data formatting | bytes 29203456 | tf_op args[3]
  66.4 0.2 pad_maximum_fusion
  66.7 1.2 copy.42.fine_ref
  67.9 0.2 copy.41
  68.2 0.9 reshape.131.coarse_ref
  69.0 78.8 %far_field.1 = f32[8,64,152]{2,1,0:T(8,128)} custom-call(s32[2844]{0:T(1024)} %constant.16.clone.tab_ref, s32[64]{0:T(128)} %constant.17.clone.start_ref, bf16[8,216,152]{2,1,0:T(8,128)(2,1)} %copy.42.fine_ref, bf16[8,64,152]{2,1,0:T(8,128)(2,1)} %reshape.131.coarse_ref, bf16[1728,216]{1,0:T(8,128)(2,1)} %constant.14.clone.sf_ref, ...), custom_call_target="tpu_custom_call" | custom-call | tf_op jit(solution)/shard_map/far_field/pallas_call | solution.py:163
  147.8 1.4 copy.44
  149.1 0.1 bitcast_select_fusion
  149.3 0.9 copy.45
  (38 shorter events, 0.5 us)
Async XLA Ops:
  0.0 2.1 %copy-start = (bf16[8,152,152]{2,1,0:T(8,128)(2,1)S(1)}, bf16[8,152,152]{2,1,0:T(8,128)(2,1)}, u32[]{:S(2)}) copy-start(bf16[8,152,152]{2,1,0:T(8,128)(2,1)} %param.11) | copy-start | bytes 1108996
  2.5 4.4 %collective-permute-start.1 = (bf16[8,20,152]{2,0,1:T(8,128)(2,1)S(1)}, bf16[8,20,152]{2,0,1:T(8,128)(2,1)S(1)}, u32[]{:S(2)}, u32[]{:S(2)}) collective-permute-start(bf16[8,20,152]{2,0,1:T(8,128)(2,1)S(1)} %pad_maximum_fusion.16), channel_id=1, source_target_pairs={{1,0},{8,1},{3,2},{10,3},{5,4},{12,5},{7,6},{14,7},{9,8},{11,10},{... | collective-permute-start | bytes 145928 | tf_op jit(solution)/shard_map/ppermute | solution.py:216
  4.5 5.8 %collective-permute-start = (bf16[8,20,152]{2,0,1:T(8,128)(2,1)S(1)}, bf16[8,20,152]{2,0,1:T(8,128)(2,1)S(1)}, u32[]{:S(2)}, u32[]{:S(2)}) collective-permute-start(bf16[8,20,152]{2,0,1:T(8,128)(2,1)S(1)} %pad_maximum_fusion.15), channel_id=1, source_target_pairs={{0,1},{1,8},{2,3},{3,10},{4,5},{5,12},{6,7},{7,14},{8,9},{10,11},{... | collective-permute-start | bytes 145928 | tf_op jit(solution)/shard_map/ppermute | solution.py:215
  10.4 6.9 %collective-permute-start.3 = (bf16[8,32,152]{2,0,1:T(8,128)(2,1)S(1)}, bf16[8,32,152]{2,0,1:T(8,128)(2,1)S(1)}, u32[]{:S(2)}, u32[]{:S(2)}) collective-permute-start(bf16[8,32,152]{2,0,1:T(8,128)(2,1)S(1)} %pad_maximum_fusion.10), channel_id=1, source_target_pairs={{2,0},{3,1},{16,2},{17,3},{6,4},{7,5},{20,6},{21,7},{10,8},{11,9},... | collective-permute-start | bytes 233480 | tf_op jit(solution)/shard_map/ppermute | solution.py:216
  13.6 9.5 %collective-permute-start.2 = (bf16[8,32,152]{2,0,1:T(8,128)(2,1)S(1)}, bf16[8,32,152]{2,0,1:T(8,128)(2,1)S(1)}, u32[]{:S(2)}, u32[]{:S(2)}) collective-permute-start(bf16[8,32,152]{2,0,1:T(8,128)(2,1)S(1)} %pad_maximum_fusion.9), channel_id=1, source_target_pairs={{0,2},{1,3},{2,16},{3,17},{4,6},{5,7},{6,20},{7,21},{8,10},{9,11},... | collective-permute-start | bytes 233480 | tf_op jit(solution)/shard_map/ppermute | solution.py:215
  23.4 43.0 %collective-permute-start.5 = (bf16[8,52,152]{2,0,1:T(8,128)(2,1)S(1)}, bf16[8,52,152]{2,0,1:T(8,128)(2,1)S(1)}, u32[]{:S(2)}, u32[]{:S(2)}) collective-permute-start(bf16[8,52,152]{2,0,1:T(8,128)(2,1)S(1)} %pad_maximum_fusion.3), channel_id=1, source_target_pairs={{4,0},{5,1},{6,2},{7,3},{12,8},{13,9},{14,10},{15,11},{20,16},{21,... | collective-permute-start | bytes 379400 | tf_op jit(solution)/shard_map/ppermute | solution.py:216
  24.8 41.7 %collective-permute-start.4 = (bf16[8,52,152]{2,0,1:T(8,128)(2,1)S(1)}, bf16[8,52,152]{2,0,1:T(8,128)(2,1)S(1)}, u32[]{:S(2)}, u32[]{:S(2)}) collective-permute-start(bf16[8,52,152]{2,0,1:T(8,128)(2,1)S(1)} %pad_maximum_fusion.2), channel_id=1, source_target_pairs={{0,4},{1,5},{2,6},{3,7},{8,12},{9,13},{10,14},{11,15},{16,20},{17,... | collective-permute-start | bytes 379400 | tf_op jit(solution)/shard_map/ppermute | solution.py:215
where the time goes:
time: 151 us; the launch traced here: 150 us
  Pallas kernels  78.8 us (52%)
  local copies, waits for them, and re-layouts  42.8 us (28%)
  starting transfers between devices  16 us (11%)
  waiting for transfers between devices  10.2 us (7%)
  other arithmetic  1.76 us (1%)
    pallas_call x1, Pallas kernels, far_field(): pl.pallas_call(functools.partial(far_kernel, slabs, nf, nc), out_shape=ja...  78.8 us
    unnamed x4, local copies, waits for them, and re-layouts  38.1 us
    ppermute x3, starting transfers between devices, exchange(): below = lax.ppermute(faces(True), 'box', up)  9.65 us
    ppermute x3, waiting for transfers between devices, exchange(): below = lax.ppermute(faces(True), 'box', up)  9.21 us
    ppermute x3, starting transfers between devices, exchange(): above = lax.ppermute(faces(False), 'box', down)  6.38 us
  transfers between devices with their start and end apart: 6, of which 3 were waited for; matrix products, arithmetic and copies ran while one was open for 25% of the time, Pallas kernels for 0%

commit v1 on v0

--- a/solution.py
+++ b/solution.py
@@ -9,6 +9,8 @@
 from jax.sharding import PartitionSpec as P
 
 PAD = 16
+GROUPS = ((8, 7), (4, 5), (2, 5), (1, 1))
+SLABS = 8
 NT_DIMS = (((1,), (1,)), ((), ()))
 
 
@@ -48,28 +50,28 @@
 
 def build_tables():
     offsets = offsets_table()
-    rows, starts, slabs = [], [], []
-    for u in range(-3, 4):
-        members = [t for t, o in enumerate(offsets) if o[0] == u]
-        slabs.append((members[0], len(members)))
-        for kv in range(3):
-            for kw in range(3):
-                starts.append(len(rows))
-                for t in members:
-                    o = offsets[t]
-                    if kind(o[1]) != kv or kind(o[2]) != kw:
-                        continue
-                    entry = [t]
-                    for k in classes_of((kind(u), kv, kw)):
+    tables = []
+    for classes, together in GROUPS:
+        rows = []
+        for kinds in np.ndindex(3, 3, 3):
+            ks = classes_of(kinds)
+            if len(ks) != classes:
+                continue
+            members = [t for t, o in enumerate(offsets) if tuple(map(kind, o)) == kinds]
+            for first in range(0, len(members), together):
+                entry = list(ks)
+                for t in members[first : first + together]:
+                    entry.append(t)
+                    for k in ks:
                         d, child = 0, 0
                         for a in range(3):
-                            s = o[a] + (k >> a & 1)
+                            s = offsets[t][a] + (k >> a & 1)
                             child |= (s & 1) << a
                             d = d * 3 + (s >> 1) + 1
                         entry.append(d * 8 + child)
-                    rows.append(entry + [0] * (9 - len(entry)))
-    starts.append(len(rows))
-    return np.array(rows, np.int32).reshape(-1), np.array(starts, np.int32), slabs
+                rows.append(entry)
+        tables.append(np.array(rows, np.int32))
+    return tables
 
 
 def selector(bit_count, pad):
@@ -87,18 +89,19 @@
 
 
 def far_kernel(
-    slabs, nf, nc, tab_ref, start_ref, fine_ref, coarse_ref, sf_ref, sc_ref, l2l_ref, m2l_ref,
+    layout, nf, nc, tab_ref, fine_ref, coarse_ref, sf_ref, sc_ref, l2l_ref, m2l_ref,
     out_ref, ops, win, acc, sems
 ):
+    total = ops.shape[0]
     copies = []
-    for i, (first, size) in enumerate(slabs):
+    for i in range(SLABS):
+        at, end = total * i // SLABS, total * (i + 1) // SLABS
         copy = pltpu.make_async_copy(
-            m2l_ref.at[pl.ds(first, size)], ops.at[pl.ds(first, size)], sems.at[i]
+            m2l_ref.at[pl.ds(at, end - at)], ops.at[pl.ds(at, end - at)], sems.at[i]
         )
         copy.start()
         copies.append(copy)
     acc[...] = jnp.zeros_like(acc)
-    points = fine_ref.shape[-1]
 
     def build(j, carry):
         f = fine_ref[j]
@@ -115,36 +118,29 @@
     lax.fori_loop(0, 8, build, 0)
     rows = nf + PAD
 
-    def slab(i, ku):
-        for kv in range(3):
-            for kw in range(3):
-                ks = classes_of((ku, kv, kw))
-
-                def step(n, carry, ks=ks):
-                    op = ops[tab_ref[n * 9]]
-                    lhs = jnp.concatenate(
-                        [win[tab_ref[n * 9 + 1 + e]] for e in range(len(ks))], axis=0
-                    )
-                    res = lax.dot_general(lhs, op, NT_DIMS, preferred_element_type=jnp.float32)
-                    for e, k in enumerate(ks):
-                        acc[k] += res[e * rows : (e + 1) * rows]
-                    return carry
-
-                at = i * 9 + kv * 3 + kw
-                lax.fori_loop(start_ref[at], start_ref[at + 1], step, 0)
-
-    copies[0].wait()
-    slab(0, 0)
-    for i in range(1, 6):
-        copies[i].wait()
-
-    def inner(i, carry):
-        slab(i, 1)
-        return carry
-
-    lax.fori_loop(1, 6, inner, 0)
-    copies[6].wait()
-    slab(6, 2)
+    for copy in copies:
+        copy.wait()
+
+    def apply(base, classes, together):
+        sums = None
+        for j in range(together):
+            at = base + classes + j * (classes + 1)
+            lhs = [win[tab_ref[at + 1 + e]] for e in range(classes)]
+            lhs = jnp.concatenate(lhs, axis=0) if classes > 1 else lhs[0]
+            term = lax.dot_general(
+                lhs, ops[tab_ref[at]], NT_DIMS, preferred_element_type=jnp.float32
+            )
+            sums = term if sums is None else sums + term
+        for e in range(classes):
+            acc[tab_ref[base + e]] += sums[e * rows : (e + 1) * rows]
+
+    for first, count, width, classes, together in layout:
+
+        def step(n, carry, first=first, width=width, classes=classes, together=together):
+            apply(first + n * width, classes, together)
+            return carry
+
+        lax.fori_loop(0, count, step, 0)
 
     down = jnp.concatenate([acc[k, nf : nf + nc, :] for k in range(8)], axis=0).astype(jnp.bfloat16)
     for k in range(8):
@@ -154,26 +150,31 @@
 
 
 def far_field(fine, coarse, m2l_ops, l2l_ops, nf, nc, local_bits):
-    tab, starts, slabs = build_tables()
+    tables = build_tables()
+    layout, at = [], 0
+    for table, (classes, together) in zip(tables, GROUPS):
+        layout.append((at,) + table.shape + (classes, together))
+        at += table.size
+    tab = np.concatenate([table.reshape(-1) for table in tables])
     points = fine.shape[-1]
     sf = jnp.asarray(selector(local_bits - 3, 0), jnp.bfloat16)
     sc = jnp.asarray(selector(local_bits - 6, PAD), jnp.bfloat16)
     vmem = pl.BlockSpec(memory_space=pltpu.VMEM)
     smem = pl.BlockSpec(memory_space=pltpu.SMEM)
     return pl.pallas_call(
-        functools.partial(far_kernel, slabs, nf, nc),
+        functools.partial(far_kernel, layout, nf, nc),
         out_shape=jax.ShapeDtypeStruct((8, nf, points), jnp.float32),
-        in_specs=[smem, smem, vmem, vmem, vmem, vmem, vmem, pl.BlockSpec(memory_space=pl.ANY)],
+        in_specs=[smem, vmem, vmem, vmem, vmem, vmem, pl.BlockSpec(memory_space=pl.ANY)],
         out_specs=vmem,
         scratch_shapes=[
             pltpu.VMEM(m2l_ops.shape, jnp.bfloat16),
             pltpu.VMEM((27 * 8, nf + PAD, points), jnp.bfloat16),
             pltpu.VMEM((8, nf + PAD, points), jnp.float32),
-            pltpu.SemaphoreType.DMA((len(slabs),)),
+            pltpu.SemaphoreType.DMA((SLABS,)),
         ],
         compiler_params=pltpu.CompilerParams(vmem_limit_bytes=60 * 2**20),
         name="far_field",
-    )(jnp.asarray(tab), jnp.asarray(starts), fine, coarse, sf, sc, l2l_ops, m2l_ops)
+    )(jnp.asarray(tab), fine, coarse, sf, sc, l2l_ops, m2l_ops)
 
 
 def to_grid(boxes, bit_count):

time: 151 us -> 111 us (0.74)
  Pallas kernels: 78.8 us -> 38.6 us
    pallas_call x1, Pallas kernels: 78.8 us -> 38.6 us  [far_field(): pl.pallas_call(functools.partial(far_kernel, layout, nf, nc), out_shape=j...]
  transfers between devices with their start and end apart: 6 -> 6, of which waited for: 3 -> 3; matrix products, arithmetic and copies ran while one was open for 25% -> 34% of each run, Pallas kernels for 0% -> 0%
where the time goes in v1:
time: 111 us; the launch traced here: 110 us
  local copies, waits for them, and re-layouts  42.8 us (39%)
  Pallas kernels  38.6 us (35%)
  starting transfers between devices  16 us (14%)
  waiting for transfers between devices  10.2 us (9%)
  other arithmetic  1.76 us (2%)
    pallas_call x1, Pallas kernels, far_field(): pl.pallas_call(functools.partial(far_kernel, layout, nf, nc), out_shape=j...  38.6 us
    unnamed x4, local copies, waits for them, and re-layouts  38.1 us
    ppermute x3, starting transfers between devices, exchange(): below = lax.ppermute(faces(True), 'box', up)  9.65 us
    ppermute x3, waiting for transfers between devices, exchange(): below = lax.ppermute(faces(True), 'box', up)  9.21 us
    ppermute x3, starting transfers between devices, exchange(): above = lax.ppermute(faces(False), 'box', down)  6.38 us
  transfers between devices with their start and end apart: 6, of which 3 were waited for; matrix products, arithmetic and copies ran while one was open for 34% of the time, Pallas kernels for 0%

profile of v1, /device:TPU:24, one launch (start us, length us, event | category | flops | bytes accessed | tf_op | source)
XLA Modules:
  0.0 110.0 jit_solution(2242995493987740972)
XLA Ops:
  0.0 0.7 broadcast_compare_fusion
  0.8 1.0 copy.25
  1.8 0.1 fusion.7
  1.9 0.1 broadcast_select_fusion
  2.1 0.3 fusion
  2.5 1.9 %collective-permute-start.1 = (bf16[8,20,152]{2,0,1:T(8,128)(2,1)S(1)}, bf16[8,20,152]{2,0,1:T(8,128)(2,1)S(1)}, u32[]{:S(2)}, u32[]{:S(2)}) collective-permute-start(bf16[8,20,152]{2,0,1:T(8,128)(2,1)S(1)} %pad_maximum_fusion.16), channel_id=1, source_target_pairs={{1,0},{8,1},{3,2},{10,3},{5,4},{12,5},{7,6},{14,7},{9,8},{11,10},{... | collective-permute-start | bytes 145928 | tf_op jit(solution)/shard_map/ppermute | solution.py:217
  4.5 2.4 %collective-permute-start = (bf16[8,20,152]{2,0,1:T(8,128)(2,1)S(1)}, bf16[8,20,152]{2,0,1:T(8,128)(2,1)S(1)}, u32[]{:S(2)}, u32[]{:S(2)}) collective-permute-start(bf16[8,20,152]{2,0,1:T(8,128)(2,1)S(1)} %pad_maximum_fusion.15), channel_id=1, source_target_pairs={{0,1},{1,8},{2,3},{3,10},{4,5},{5,12},{6,7},{7,14},{8,9},{10,11},{... | collective-permute-start | bytes 145928 | tf_op jit(solution)/shard_map/ppermute | solution.py:216
  6.9 3.3 %collective-permute-done = bf16[8,20,152]{2,0,1:T(8,128)(2,1)S(1)} collective-permute-done((bf16[8,20,152]{2,0,1:T(8,128)(2,1)S(1)}, bf16[8,20,152]{2,0,1:T(8,128)(2,1)S(1)}, u32[]{:S(2)}, u32[]{:S(2)}) %collective-permute-start) | collective-permute-done | bytes 48672 | tf_op jit(solution)/shard_map/ppermute | solution.py:216
  10.4 3.2 %collective-permute-start.3 = (bf16[8,32,152]{2,0,1:T(8,128)(2,1)S(1)}, bf16[8,32,152]{2,0,1:T(8,128)(2,1)S(1)}, u32[]{:S(2)}, u32[]{:S(2)}) collective-permute-start(bf16[8,32,152]{2,0,1:T(8,128)(2,1)S(1)} %pad_maximum_fusion.10), channel_id=1, source_target_pairs={{2,0},{3,1},{16,2},{17,3},{6,4},{7,5},{20,6},{21,7},{10,8},{11,9},... | collective-permute-start | bytes 233480 | tf_op jit(solution)/shard_map/ppermute | solution.py:217
  13.6 2.7 %collective-permute-start.2 = (bf16[8,32,152]{2,0,1:T(8,128)(2,1)S(1)}, bf16[8,32,152]{2,0,1:T(8,128)(2,1)S(1)}, u32[]{:S(2)}, u32[]{:S(2)}) collective-permute-start(bf16[8,32,152]{2,0,1:T(8,128)(2,1)S(1)} %pad_maximum_fusion.9), channel_id=1, source_target_pairs={{0,2},{1,3},{2,16},{3,17},{4,6},{5,7},{6,20},{7,21},{8,10},{9,11},... | collective-permute-start | bytes 233480 | tf_op jit(solution)/shard_map/ppermute | solution.py:216
  16.3 1.0 collective-permute-done.3
  17.3 5.9 %collective-permute-done.2 = bf16[8,32,152]{2,0,1:T(8,128)(2,1)S(1)} collective-permute-done((bf16[8,32,152]{2,0,1:T(8,128)(2,1)S(1)}, bf16[8,32,152]{2,0,1:T(8,128)(2,1)S(1)}, u32[]{:S(2)}, u32[]{:S(2)}) %collective-permute-start.2) | collective-permute-done | bytes 77856 | tf_op jit(solution)/shard_map/ppermute | solution.py:216
  23.3 0.1 pad_maximum_fusion.8
  23.4 1.3 %collective-permute-start.5 = (bf16[8,52,152]{2,0,1:T(8,128)(2,1)S(1)}, bf16[8,52,152]{2,0,1:T(8,128)(2,1)S(1)}, u32[]{:S(2)}, u32[]{:S(2)}) collective-permute-start(bf16[8,52,152]{2,0,1:T(8,128)(2,1)S(1)} %pad_maximum_fusion.3), channel_id=1, source_target_pairs={{4,0},{5,1},{6,2},{7,3},{12,8},{13,9},{14,10},{15,11},{20,16},{21,... | collective-permute-start | bytes 379400 | tf_op jit(solution)/shard_map/ppermute | solution.py:217
  24.8 4.6 %collective-permute-start.4 = (bf16[8,52,152]{2,0,1:T(8,128)(2,1)S(1)}, bf16[8,52,152]{2,0,1:T(8,128)(2,1)S(1)}, u32[]{:S(2)}, u32[]{:S(2)}) collective-permute-start(bf16[8,52,152]{2,0,1:T(8,128)(2,1)S(1)} %pad_maximum_fusion.2), channel_id=1, source_target_pairs={{0,4},{1,5},{2,6},{3,7},{8,12},{9,13},{10,14},{11,15},{16,20},{17,... | collective-permute-start | bytes 379400 | tf_op jit(solution)/shard_map/ppermute | solution.py:216
  29.3 37.1 %copy.42.m2l_ref = bf16[316,152,152]{2,1,0:T(8,128)(2,1)} copy(bf16[316,152,152]{0,2,1:T(8,128)(2,1)} %param.11) | data formatting | bytes 29203456 | tf_op args[3]
  66.4 0.2 pad_maximum_fusion
  66.7 1.2 %copy.41.fine_ref = bf16[8,216,152]{2,1,0:T(8,128)(2,1)} copy(bf16[8,216,152]{2,0,1:T(8,128)(2,1)S(1)} %bitcast.55) | data formatting | bytes 1050624 | tf_op jit(solution)/shard_map/reshape | solution.py:254
  67.9 0.2 copy.40
  68.2 0.9 reshape.131.coarse_ref
  69.0 38.6 %far_field.1 = f32[8,64,152]{2,1,0:T(8,128)} custom-call(s32[2092]{0:T(1024)} %constant.14.clone.tab_ref, bf16[8,216,152]{2,1,0:T(8,128)(2,1)} %copy.41.fine_ref, bf16[8,64,152]{2,1,0:T(8,128)(2,1)} %reshape.131.coarse_ref, bf16[1728,216]{1,0:T(8,128)(2,1)} %constant.12.clone.sf_ref, bf16[432,64]{1,0:T(8,128)(2,1)} %constant.13.clone.sc_ref, ...), custom_call_target="tpu_custom_call" | custom-call | tf_op jit(solution)/shard_map/far_field/pallas_call | solution.py:164
  107.6 1.4 %copy.43 = f32[8,8,8,152]{3,0,1,2:T(8,128)S(1)} copy(f32[8,8,8,152]{3,2,1,0:T(8,128)} %bitcast.56) | data formatting | bytes 622592 | tf_op jit(solution)/shard_map/reshape | solution.py:256
  109.0 0.1 bitcast_select_fusion
  109.1 0.9 copy.44
  (38 shorter events, 0.5 us)
Async XLA Ops:
  0.0 2.1 %copy-start = (bf16[8,152,152]{2,1,0:T(8,128)(2,1)S(1)}, bf16[8,152,152]{2,1,0:T(8,128)(2,1)}, u32[]{:S(2)}) copy-start(bf16[8,152,152]{2,1,0:T(8,128)(2,1)} %param.10) | copy-start | bytes 1108996
  2.5 4.4 %collective-permute-start.1 = (bf16[8,20,152]{2,0,1:T(8,128)(2,1)S(1)}, bf16[8,20,152]{2,0,1:T(8,128)(2,1)S(1)}, u32[]{:S(2)}, u32[]{:S(2)}) collective-permute-start(bf16[8,20,152]{2,0,1:T(8,128)(2,1)S(1)} %pad_maximum_fusion.16), channel_id=1, source_target_pairs={{1,0},{8,1},{3,2},{10,3},{5,4},{12,5},{7,6},{14,7},{9,8},{11,10},{... | collective-permute-start | bytes 145928 | tf_op jit(solution)/shard_map/ppermute | solution.py:217
  4.5 5.8 %collective-permute-start = (bf16[8,20,152]{2,0,1:T(8,128)(2,1)S(1)}, bf16[8,20,152]{2,0,1:T(8,128)(2,1)S(1)}, u32[]{:S(2)}, u32[]{:S(2)}) collective-permute-start(bf16[8,20,152]{2,0,1:T(8,128)(2,1)S(1)} %pad_maximum_fusion.15), channel_id=1, source_target_pairs={{0,1},{1,8},{2,3},{3,10},{4,5},{5,12},{6,7},{7,14},{8,9},{10,11},{... | collective-permute-start | bytes 145928 | tf_op jit(solution)/shard_map/ppermute | solution.py:216
  10.4 6.9 %collective-permute-start.3 = (bf16[8,32,152]{2,0,1:T(8,128)(2,1)S(1)}, bf16[8,32,152]{2,0,1:T(8,128)(2,1)S(1)}, u32[]{:S(2)}, u32[]{:S(2)}) collective-permute-start(bf16[8,32,152]{2,0,1:T(8,128)(2,1)S(1)} %pad_maximum_fusion.10), channel_id=1, source_target_pairs={{2,0},{3,1},{16,2},{17,3},{6,4},{7,5},{20,6},{21,7},{10,8},{11,9},... | collective-permute-start | bytes 233480 | tf_op jit(solution)/shard_map/ppermute | solution.py:217
  13.6 9.5 %collective-permute-start.2 = (bf16[8,32,152]{2,0,1:T(8,128)(2,1)S(1)}, bf16[8,32,152]{2,0,1:T(8,128)(2,1)S(1)}, u32[]{:S(2)}, u32[]{:S(2)}) collective-permute-start(bf16[8,32,152]{2,0,1:T(8,128)(2,1)S(1)} %pad_maximum_fusion.9), channel_id=1, source_target_pairs={{0,2},{1,3},{2,16},{3,17},{4,6},{5,7},{6,20},{7,21},{8,10},{9,11},... | collective-permute-start | bytes 233480 | tf_op jit(solution)/shard_map/ppermute | solution.py:216
  23.4 43.0 %collective-permute-start.5 = (bf16[8,52,152]{2,0,1:T(8,128)(2,1)S(1)}, bf16[8,52,152]{2,0,1:T(8,128)(2,1)S(1)}, u32[]{:S(2)}, u32[]{:S(2)}) collective-permute-start(bf16[8,52,152]{2,0,1:T(8,128)(2,1)S(1)} %pad_maximum_fusion.3), channel_id=1, source_target_pairs={{4,0},{5,1},{6,2},{7,3},{12,8},{13,9},{14,10},{15,11},{20,16},{21,... | collective-permute-start | bytes 379400 | tf_op jit(solution)/shard_map/ppermute | solution.py:217
  24.8 41.7 %collective-permute-start.4 = (bf16[8,52,152]{2,0,1:T(8,128)(2,1)S(1)}, bf16[8,52,152]{2,0,1:T(8,128)(2,1)S(1)}, u32[]{:S(2)}, u32[]{:S(2)}) collective-permute-start(bf16[8,52,152]{2,0,1:T(8,128)(2,1)S(1)} %pad_maximum_fusion.2), channel_id=1, source_target_pairs={{0,4},{1,5},{2,6},{3,7},{8,12},{9,13},{10,14},{11,15},{16,20},{17,... | collective-permute-start | bytes 379400 | tf_op jit(solution)/shard_map/ppermute | solution.py:216

commit v2 on v1

--- a/solution.py
+++ b/solution.py
@@ -106,13 +106,15 @@
     def build(j, carry):
         f = fine_ref[j]
         c = coarse_ref[j]
+        for d in range(0, 27, 9):
+            part = jnp.dot(
+                sf_ref[d * nf : (d + 9) * nf, :], f, preferred_element_type=jnp.float32
+            ).astype(jnp.bfloat16)
+            for e in range(9):
+                win[(d + e) * 8 + j, 0:nf, :] = part[e * nf : (e + 1) * nf]
+        part = jnp.dot(sc_ref[...], c, preferred_element_type=jnp.float32).astype(jnp.bfloat16)
         for d in range(27):
-            win[d * 8 + j, 0:nf, :] = jnp.dot(
-                sf_ref[d * nf : (d + 1) * nf, :], f, preferred_element_type=jnp.float32
-            ).astype(jnp.bfloat16)
-            win[d * 8 + j, nf : nf + PAD, :] = jnp.dot(
-                sc_ref[d * PAD : (d + 1) * PAD, :], c, preferred_element_type=jnp.float32
-            ).astype(jnp.bfloat16)
+            win[d * 8 + j, nf : nf + PAD, :] = part[d * PAD : (d + 1) * PAD]
         return carry
 
     lax.fori_loop(0, 8, build, 0)
@@ -178,61 +180,97 @@
 
 
 def to_grid(boxes, bit_count):
-    lead, count, points = boxes.shape
-    bitwise = boxes.reshape((lead,) + (2,) * bit_count + (points,))
-    order = [0]
+    bitwise = boxes.reshape((2,) * bit_count + boxes.shape[1:])
+    order = []
     for a in range(3):
-        order += [bit_count - i for i in range(bit_count) if i % 3 == a][::-1]
-    return bitwise.transpose(order + [bit_count + 1]).reshape([lead] + extents(bit_count) + [points])
-
-
-def neighbours(devices, device_bits, local_bits, axis):
-    members = [p for p in range(device_bits) if (local_bits + p) % 3 == axis]
-    pairs = []
-    for i in range(devices):
-        coord = sum((i >> p & 1) << n for n, p in enumerate(members))
-        if coord + 1 < 2 ** len(members):
-            j = i
+        order += [bit_count - 1 - i for i in range(bit_count) if i % 3 == a][::-1]
+    order += [bit_count, bit_count + 1]
+    return bitwise.transpose(order).reshape(extents(bit_count) + list(boxes.shape[1:]))
+
+
+def halo_kernel(device_bits, local_bits, *refs):
+    blocks, outs, grids = refs[0:2], refs[2:4], refs[4:6]
+    send_sems, recv_sems = refs[6:8]
+    me = lax.axis_index("box")
+    ways = []
+    for axis in range(3):
+        members = [p for p in range(device_bits) if (local_bits + p) % 3 == axis]
+        bits = [lax.rem(lax.div(me, 1 << p), 2) for p in members]
+        here = sum((bit * (1 << n) for n, bit in enumerate(bits)), jnp.int32(0))
+        size = 1 << len(members)
+
+        def device_at(coord):
+            out = me
             for n, p in enumerate(members):
-                j = j & ~(1 << p) | ((coord + 1) >> n & 1) << p
-            pairs.append((i, j))
-    return pairs
-
-
-def exchange(grids, devices, device_bits, local_bits):
+                out = out + (lax.rem(lax.div(coord, 1 << n), 2) - bits[n]) * (1 << p)
+            return out
+
+        ways.append(
+            (
+                (here < size - 1, device_at(here + 1)),
+                (here > 0, device_at(here + (size - 1))),
+            )
+        )
+    for block, grid in zip(blocks, grids):
+        grid[...] = jnp.zeros_like(grid)
+        x, y, z = block.shape[:3]
+        grid[1 : x + 1, 1 : y + 1, 1 : z + 1] = block[...]
+    barrier = pltpu.get_barrier_semaphore()
+    flat = [way for pair in ways for way in pair]
+    for there, device in flat:
+
+        @pl.when(there)
+        def _(device=device):
+            pl.semaphore_signal(
+                barrier, inc=1, device_id=(device,), device_id_type=pl.DeviceIdType.MESH
+            )
+
+    peers = sum((jnp.where(there, 1, 0) for there, _ in flat), jnp.int32(0))
+    pl.semaphore_wait(barrier, peers)
+
     for axis in range(3):
-        up = neighbours(devices, device_bits, local_bits, axis)
-        down = [(j, i) for i, j in up]
-        dim = axis + 1
-
-        def faces(at_top):
-            cut = []
-            for g in grids:
-                s = g.shape[dim] - 1 if at_top else 0
-                face = lax.slice_in_dim(g, s, s + 1, axis=dim)
-                cut.append(face.reshape(g.shape[0], -1, g.shape[-1]))
-            return jnp.concatenate(cut, axis=1)
-
-        below = lax.ppermute(faces(True), "box", up)
-        above = lax.ppermute(faces(False), "box", down)
-        out, at = [], 0
-        for g in grids:
-            shape = list(g.shape)
-            shape[dim] = 1
-            size = shape[1] * shape[2] * shape[3]
-            out.append(
-                jnp.concatenate(
-                    [
-                        below[:, at : at + size].reshape(shape),
-                        g,
-                        above[:, at : at + size].reshape(shape),
-                    ],
-                    axis=dim,
+        moves = []
+        for way in range(2):
+            for n, grid in enumerate(grids):
+                extent = [e - 2 for e in grid.shape[:3]]
+                region = [
+                    pl.ds(0, extent[a] + 2) if a < axis else pl.ds(1, extent[a]) for a in range(3)
+                ]
+                source, target = list(region), list(region)
+                source[axis] = pl.ds(extent[axis] if way == 0 else 1, 1)
+                target[axis] = pl.ds(0 if way == 0 else extent[axis] + 1, 1)
+                at = (axis * 2 + way) * 2 + n
+                copy = pltpu.make_async_remote_copy(
+                    src_ref=grid.at[tuple(source)],
+                    dst_ref=grid.at[tuple(target)],
+                    send_sem=send_sems.at[at],
+                    recv_sem=recv_sems.at[at],
+                    device_id=(ways[axis][way][1],),
+                    device_id_type=pl.DeviceIdType.MESH,
                 )
-            )
-            at += size
-        grids = out
-    return grids
+                moves.append((way, copy))
+        for way, copy in moves:
+            pl.when(ways[axis][way][0])(copy.start)
+        for way, copy in moves:
+            pl.when(ways[axis][way][0])(copy.wait_send)
+            pl.when(ways[axis][1 - way][0])(copy.wait_recv)
+    for grid, out in zip(grids, outs):
+        out[...] = grid[...]
+
+
+def exchange(blocks, device_bits, local_bits):
+    shapes = [tuple(e + 2 for e in b.shape[:3]) + b.shape[3:] for b in blocks]
+    vmem = pl.BlockSpec(memory_space=pltpu.VMEM)
+    return pl.pallas_call(
+        functools.partial(halo_kernel, device_bits, local_bits),
+        out_shape=[jax.ShapeDtypeStruct(shape, jnp.bfloat16) for shape in shapes],
+        in_specs=[vmem, vmem],
+        out_specs=[vmem, vmem],
+        scratch_shapes=[pltpu.VMEM(shape, jnp.bfloat16) for shape in shapes]
+        + [pltpu.SemaphoreType.DMA((12,)), pltpu.SemaphoreType.DMA((12,))],
+        compiler_params=pltpu.CompilerParams(collective_id=0, has_side_effects=True),
+        name="halo",
+    )(*blocks)
 
 
 def shards(fine_multipoles, present, m2m_ops, m2l_ops, l2l_ops):
@@ -242,16 +280,15 @@
     device_bits = devices.bit_length() - 1
     nf, nc = width // 8, width // 64
     masked = jnp.where(present[None, :] > 0, fine_multipoles, jnp.zeros_like(fine_multipoles))
-    fine = masked.reshape(points, nf, 8).transpose(2, 1, 0)
+    fine = masked.T.reshape(nf, 8, points)
     coarse = jnp.einsum(
-        "kcq,kpq->cp", fine, m2m_ops, preferred_element_type=jnp.float32
+        "ckq,kpq->cp", fine, m2m_ops, preferred_element_type=jnp.float32
     ).astype(jnp.bfloat16)
-    coarse = coarse.reshape(nc, 8, points).transpose(1, 0, 2)
     grids = exchange(
-        [to_grid(fine, local_bits - 3), to_grid(coarse, local_bits - 6)],
-        devices, device_bits, local_bits,
+        [to_grid(fine, local_bits - 3), to_grid(coarse.reshape(nc, 8, points), local_bits - 6)],
+        device_bits, local_bits,
     )
-    flat = [g.reshape(8, -1, points) for g in grids]
+    flat = [g.reshape(-1, 8, points).transpose(1, 0, 2) for g in grids]
     rows = far_field(flat[0], flat[1], m2l_ops, l2l_ops, nf, nc, local_bits)
     out = rows.reshape(8, 8, nc, points).transpose(3, 2, 1, 0).reshape(points, width)
     return jnp.where(present[None, :] > 0, out, 0.0)

time: 111 us -> 108 us (0.973)
  Pallas kernels: 38.6 us -> 59.2 us
  starting transfers between devices: 16 us -> 0 us
  waiting for transfers between devices: 10.2 us -> 0 us
  local copies, waits for them, and re-layouts: 42.8 us -> 45.7 us
    pallas_call x0 -> x1, Pallas kernels: none -> 20.6 us  [exchange(): pl.pallas_call(functools.partial(halo_kernel, device_bits, local_bits), o...]
    ppermute x6 -> x0, starting transfers between devices: 16 us -> none  [the longest x3 9.65 us: exchange(): below = lax.ppermute(faces(True), 'box', up)]
    ppermute x6 -> x0, waiting for transfers between devices: 10.2 us -> none  [the longest x3 9.21 us: exchange(): below = lax.ppermute(faces(True), 'box', up)]
    reshape x2, local copies, waits for them, and re-layouts: 2.05 us -> 4.03 us  [shards(): flat = [g.reshape(-1, 8, points).transpose(1, 0, 2) for g in grids]]
  transfers between devices with their start and end apart: 6 -> 0, of which waited for: 3 -> 0; matrix products, arithmetic and copies ran while one was open for 34% -> 0% of each run, Pallas kernels for 0% -> 0%
where the time goes in v2:
time: 108 us; the launch traced here: 107 us
  Pallas kernels  59.2 us (55%)
  local copies, waits for them, and re-layouts  45.7 us (42%)
  other arithmetic  1.15 us (1%)
    pallas_call x1, Pallas kernels, far_field(): pl.pallas_call(functools.partial(far_kernel, layout, nf, nc), out_shape=j...  38.6 us
    unnamed x4, local copies, waits for them, and re-layouts  38.1 us
    pallas_call x1, Pallas kernels, exchange(): pl.pallas_call(functools.partial(halo_kernel, device_bits, local_bits), o...  20.6 us
    reshape x2, local copies, waits for them, and re-layouts, shards(): flat = [g.reshape(-1, 8, points).transpose(1, 0, 2) for g in grids]  4.03 us

profile of v2, /device:TPU:24, one launch (start us, length us, event | category | flops | bytes accessed | tf_op | source)
XLA Modules:
  0.0 106.5 jit_solution(5613296006473691403)
XLA Ops:
  0.0 0.0 copy-start
  0.0 0.7 broadcast_compare_fusion
  0.8 1.0 copy.15
  1.8 0.1 fusion.3
  1.9 0.0 copy-done
  2.0 0.3 fusion
  2.3 0.6 copy.32
  2.9 0.1 broadcast_select_fusion
  3.0 0.7 copy.16
  3.8 20.6 %halo.1 = (bf16[6,6,6,8,152]{4,3,2,1,0:T(8,128)(2,1)}, bf16[4,4,4,8,152]{4,3,2,1,0:T(8,128)(2,1)}) custom-call(bf16[4,4,4,8,152]{4,3,2,1,0:T(8,128)(2,1)} %bitcast.35, bf16[2,2,2,8,152]{4,3,2,1,0:T(8,128)(2,1)} %bitcast.38), custom_call_target="tpu_custom_call" | custom-call | tf_op jit(solution)/shard_map/halo/pallas_call | solution.py:264
  24.4 2.3 %copy.30 = bf16[216,8,152]{2,0,1:T(8,128)(2,1)} copy(bf16[216,8,152]{2,1,0:T(8,128)(2,1)} %bitcast.36) | data formatting | bytes 1050624 | tf_op jit(solution)/shard_map/reshape | solution.py:291
  26.7 1.7 %copy.31 = bf16[64,8,152]{2,0,1:T(8,128)(2,1)} copy(bf16[64,8,152]{2,1,0:T(8,128)(2,1)} %bitcast.37) | data formatting | bytes 311296 | tf_op jit(solution)/shard_map/reshape | solution.py:291
  28.4 37.1 %copy.21.m2l_ref = bf16[316,152,152]{2,1,0:T(8,128)(2,1)} copy(bf16[316,152,152]{0,2,1:T(8,128)(2,1)} %param.11) | data formatting | bytes 29203456 | tf_op args[3]
  65.5 38.6 %far_field.1 = f32[8,64,152]{2,1,0:T(8,128)} custom-call(s32[2092]{0:T(1024)} %constant.14.clone.tab_ref, bf16[8,216,152]{2,1,0:T(8,128)(2,1)} %bitcast.31, bf16[8,64,152]{2,1,0:T(8,128)(2,1)} %bitcast.33, bf16[1728,216]{1,0:T(8,128)(2,1)} %constant.12.clone.sf_ref, bf16[432,64]{1,0:T(8,128)(2,1)} %constant.13.clone.sc_ref, bf16[8,152,152]{2,1,0:T(8,128)(2,1)} %l2l_ref.1, ...), custom_call_target="tpu_custom_call" | custom-call | tf_op jit(solution)/shard_map/far_field/pallas_call | solution.py:166
  104.1 1.4 %copy.22 = f32[8,8,8,152]{3,0,1,2:T(8,128)S(1)} copy(f32[8,8,8,152]{3,2,1,0:T(8,128)} %bitcast.32) | data formatting | bytes 622592 | tf_op jit(solution)/shard_map/reshape | solution.py:293
  105.5 0.1 bitcast_select_fusion
  105.6 0.9 copy.23
Async XLA Ops:
  0.0 1.9 %copy-start = (bf16[8,152,152]{2,1,0:T(8,128)(2,1)S(1)}, bf16[8,152,152]{2,1,0:T(8,128)(2,1)}, u32[]{:S(2)}) copy-start(bf16[8,152,152]{2,1,0:T(8,128)(2,1)} %param.10) | copy-start | bytes 1108996

commit v3 on v2

--- a/solution.py
+++ b/solution.py
@@ -10,7 +10,6 @@
 
 PAD = 16
 GROUPS = ((8, 7), (4, 5), (2, 5), (1, 1))
-SLABS = 8
 NT_DIMS = (((1,), (1,)), ((), ()))
 
 
@@ -50,14 +49,19 @@
 
 def build_tables():
     offsets = offsets_table()
-    tables = []
-    for classes, together in GROUPS:
-        rows = []
+    slabs = []
+    for u in range(-3, 4):
+        members = [t for t, o in enumerate(offsets) if o[0] == u]
+        slabs.append((members[0], len(members)))
+    steps = {(u, g): [] for u in range(7) for g in range(len(GROUPS))}
+    for g, (classes, together) in enumerate(GROUPS):
         for kinds in np.ndindex(3, 3, 3):
             ks = classes_of(kinds)
             if len(ks) != classes:
                 continue
             members = [t for t, o in enumerate(offsets) if tuple(map(kind, o)) == kinds]
+            if classes < 8:
+                members.sort(key=lambda t: (offsets[t][0], t))
             for first in range(0, len(members), together):
                 entry = list(ks)
                 for t in members[first : first + together]:
@@ -69,9 +73,13 @@
                             child |= (s & 1) << a
                             d = d * 3 + (s >> 1) + 1
                         entry.append(d * 8 + child)
-                rows.append(entry)
-        tables.append(np.array(rows, np.int32))
-    return tables
+                last = max(members[first : first + together])
+                steps[offsets[last][0] + 3, g].append(entry)
+    table, starts = [], []
+    for key in sorted(steps):
+        starts += [len(table), len(steps[key])]
+        table += sum(steps[key], [])
+    return np.array(table, np.int32), np.array(starts, np.int32), slabs
 
 
 def selector(bit_count, pad):
@@ -89,15 +97,13 @@
 
 
 def far_kernel(
-    layout, nf, nc, tab_ref, fine_ref, coarse_ref, sf_ref, sc_ref, l2l_ref, m2l_ref,
+    slabs, nf, nc, tab_ref, start_ref, fine_ref, coarse_ref, sf_ref, sc_ref, l2l_ref, m2l_ref,
     out_ref, ops, win, acc, sems
 ):
-    total = ops.shape[0]
     copies = []
-    for i in range(SLABS):
-        at, end = total * i // SLABS, total * (i + 1) // SLABS
+    for i, (first, size) in enumerate(slabs):
         copy = pltpu.make_async_copy(
-            m2l_ref.at[pl.ds(at, end - at)], ops.at[pl.ds(at, end - at)], sems.at[i]
+            m2l_ref.at[pl.ds(first, size)], ops.at[pl.ds(first, size)], sems.at[i]
         )
         copy.start()
         copies.append(copy)
@@ -120,9 +126,6 @@
     lax.fori_loop(0, 8, build, 0)
     rows = nf + PAD
 
-    for copy in copies:
-        copy.wait()
-
     def apply(base, classes, together):
         sums = None
         for j in range(together):
@@ -136,13 +139,21 @@
         for e in range(classes):
             acc[tab_ref[base + e]] += sums[e * rows : (e + 1) * rows]
 
-    for first, count, width, classes, together in layout:
-
-        def step(n, carry, first=first, width=width, classes=classes, together=together):
-            apply(first + n * width, classes, together)
-            return carry
-
-        lax.fori_loop(0, count, step, 0)
+    def slab_body(slab, carry):
+        for i, copy in enumerate(copies):
+            pl.when(slab == i)(copy.wait)
+        for g, (classes, together) in enumerate(GROUPS):
+            at = (slab * len(GROUPS) + g) * 2
+            first = start_ref[at]
+
+            def step(n, carry, first=first, classes=classes, together=together):
+                apply(first + n * (classes + together * (classes + 1)), classes, together)
+                return carry
+
+            lax.fori_loop(0, start_ref[at + 1], step, 0)
+        return carry
+
+    lax.fori_loop(0, len(slabs), slab_body, 0)
 
     down = jnp.concatenate([acc[k, nf : nf + nc, :] for k in range(8)], axis=0).astype(jnp.bfloat16)
     for k in range(8):
@@ -152,31 +163,26 @@
 
 
 def far_field(fine, coarse, m2l_ops, l2l_ops, nf, nc, local_bits):
-    tables = build_tables()
-    layout, at = [], 0
-    for table, (classes, together) in zip(tables, GROUPS):
-        layout.append((at,) + table.shape + (classes, together))
-        at += table.size
-    tab = np.concatenate([table.reshape(-1) for table in tables])
+    tab, starts, slabs = build_tables()
     points = fine.shape[-1]
     sf = jnp.asarray(selector(local_bits - 3, 0), jnp.bfloat16)
     sc = jnp.asarray(selector(local_bits - 6, PAD), jnp.bfloat16)
     vmem = pl.BlockSpec(memory_space=pltpu.VMEM)
     smem = pl.BlockSpec(memory_space=pltpu.SMEM)
     return pl.pallas_call(
-        functools.partial(far_kernel, layout, nf, nc),
+        functools.partial(far_kernel, slabs, nf, nc),
         out_shape=jax.ShapeDtypeStruct((8, nf, points), jnp.float32),
-        in_specs=[smem, vmem, vmem, vmem, vmem, vmem, pl.BlockSpec(memory_space=pl.ANY)],
+        in_specs=[smem, smem, vmem, vmem, vmem, vmem, vmem, pl.BlockSpec(memory_space=pl.ANY)],
         out_specs=vmem,
         scratch_shapes=[
             pltpu.VMEM(m2l_ops.shape, jnp.bfloat16),
             pltpu.VMEM((27 * 8, nf + PAD, points), jnp.bfloat16),
             pltpu.VMEM((8, nf + PAD, points), jnp.float32),
-            pltpu.SemaphoreType.DMA((SLABS,)),
+            pltpu.SemaphoreType.DMA((len(slabs),)),
         ],
         compiler_params=pltpu.CompilerParams(vmem_limit_bytes=60 * 2**20),
         name="far_field",
-    )(jnp.asarray(tab), fine, coarse, sf, sc, l2l_ops, m2l_ops)
+    )(jnp.asarray(tab), jnp.asarray(starts), fine, coarse, sf, sc, l2l_ops, m2l_ops)
 
 
 def to_grid(boxes, bit_count):

time: 108 us -> 104 us (0.963)
  Pallas kernels: 59.2 us -> 55.2 us
    pallas_call x1, Pallas kernels: 38.6 us -> 34.5 us  [far_field(): pl.pallas_call(functools.partial(far_kernel, slabs, nf, nc), out_shape=ja...]
where the time goes in v3:
time: 104 us; the launch traced here: 102 us
  Pallas kernels  55.2 us (53%)
  local copies, waits for them, and re-layouts  45.7 us (44%)
  other arithmetic  1.15 us (1%)
    unnamed x4, local copies, waits for them, and re-layouts  38.1 us
    pallas_call x1, Pallas kernels, far_field(): pl.pallas_call(functools.partial(far_kernel, slabs, nf, nc), out_shape=ja...  34.5 us
    pallas_call x1, Pallas kernels, exchange(): pl.pallas_call(functools.partial(halo_kernel, device_bits, local_bits), o...  20.6 us
    reshape x2, local copies, waits for them, and re-layouts, shards(): flat = [g.reshape(-1, 8, points).transpose(1, 0, 2) for g in grids]  4.03 us

profile of v3, /device:TPU:24, one launch (start us, length us, event | category | flops | bytes accessed | tf_op | source)
XLA Modules:
  0.0 102.4 jit_solution(2298713826539578)
XLA Ops:
  0.0 0.0 copy-start
  0.0 0.7 broadcast_compare_fusion
  0.8 1.0 %copy.16 = bf16[152,512]{0,1:T(8,128)(2,1)S(1)} copy(bf16[152,512]{1,0:T(8,128)(2,1)} %param.9) | data formatting | bytes 311296 | tf_op args[0]
  1.8 0.1 fusion.3
  1.9 0.0 copy-done
  2.0 0.3 fusion
  2.3 0.6 copy.33
  2.9 0.1 broadcast_select_fusion
  3.0 0.7 copy.17
  3.8 20.6 %halo.1 = (bf16[6,6,6,8,152]{4,3,2,1,0:T(8,128)(2,1)}, bf16[4,4,4,8,152]{4,3,2,1,0:T(8,128)(2,1)}) custom-call(bf16[4,4,4,8,152]{4,3,2,1,0:T(8,128)(2,1)} %bitcast.35, bf16[2,2,2,8,152]{4,3,2,1,0:T(8,128)(2,1)} %bitcast.38), custom_call_target="tpu_custom_call" | custom-call | tf_op jit(solution)/shard_map/halo/pallas_call | solution.py:270
  24.4 2.3 %copy.31 = bf16[216,8,152]{2,0,1:T(8,128)(2,1)} copy(bf16[216,8,152]{2,1,0:T(8,128)(2,1)} %bitcast.36) | data formatting | bytes 1050624 | tf_op jit(solution)/shard_map/reshape | solution.py:297
  26.7 1.7 %copy.32 = bf16[64,8,152]{2,0,1:T(8,128)(2,1)} copy(bf16[64,8,152]{2,1,0:T(8,128)(2,1)} %bitcast.37) | data formatting | bytes 311296 | tf_op jit(solution)/shard_map/reshape | solution.py:297
  28.4 37.1 %copy.22.m2l_ref = bf16[316,152,152]{2,1,0:T(8,128)(2,1)} copy(bf16[316,152,152]{0,2,1:T(8,128)(2,1)} %param.12) | data formatting | bytes 29203456 | tf_op args[3]
  65.5 34.5 %far_field.1 = f32[8,64,152]{2,1,0:T(8,128)} custom-call(s32[2092]{0:T(1024)} %constant.16.clone.tab_ref, s32[56]{0:T(128)} %constant.17.clone.start_ref, bf16[8,216,152]{2,1,0:T(8,128)(2,1)} %bitcast.31, bf16[8,64,152]{2,1,0:T(8,128)(2,1)} %bitcast.33, bf16[1728,216]{1,0:T(8,128)(2,1)} %constant.14.clone.sf_ref, bf16[432,64]{1,0:T(8,128)(2,1)} %constant.15.clone.sc_ref, ...), custom_call_target="tpu_custom_call" | custom-call | tf_op jit(solution)/shard_map/far_field/pallas_call | solution.py:172
  100.0 1.4 %copy.23 = f32[8,8,8,152]{3,0,1,2:T(8,128)S(1)} copy(f32[8,8,8,152]{3,2,1,0:T(8,128)} %bitcast.32) | data formatting | bytes 622592 | tf_op jit(solution)/shard_map/reshape | solution.py:299
  101.4 0.1 bitcast_select_fusion
  101.5 0.9 copy.24
Async XLA Ops:
  0.0 1.9 %copy-start = (bf16[8,152,152]{2,1,0:T(8,128)(2,1)S(1)}, bf16[8,152,152]{2,1,0:T(8,128)(2,1)}, u32[]{:S(2)}) copy-start(bf16[8,152,152]{2,1,0:T(8,128)(2,1)} %param.11) | copy-start | bytes 1108996
